TPU v7x, 256 devices: a whole 4x4x8 slice. The times are simulated.
256 devices in a mesh: scan: 32 (over x, y, z_lo), col: 8 (over z_hi, core).
Axes of the slice: x: 4, y: 4, z: 8 (z_hi: 4, z_lo: 2; z = z_hi * 2 + z_lo), core: 2. Of those that a mesh axis runs over, the one named last changes fastest.
Arguments:
- frames: float32 [512, 128, 2048], P('scan', None, 'col'), may hold values from -6 to 6
- depth_offset: int32 [128], replicated, may hold values from -128 to 128
- band_width: int32 [128], replicated, may hold values from 1 to 8
- edge_level: int32 [128, 2048], P(None, 'col'), may hold values from 1 to 16
Outputs:
- volume: float32 [512, 128, 2048], P('scan', None, 'col')
All inputs are finite; a program needn't handle non-finite values.
Results may differ from a plain program's by a relative error of at most 0.0003.
Values sent between devices are 32-bit elements; how exact they have to be, the bound alone decides.
No kernel may reach another device: no remote copies, remote signals or barrier semaphores. Data moves between devices by JAX's collectives and lax.ppermute only.
A program may use at most 64 MiB of HBM per device.

v0:
```python
import math

import jax
import jax.numpy as jnp
from jax import lax
from jax.sharding import PartitionSpec as P

SWEEPS = 6
DIFFUSE = 6


TEMPORAL_KAPPA = 1.0
STEP_SIZE = 0.24
LEVEL_SCALE = 16.0


def diffuse_once(field, kappa, live_mask):
    change = (field[1:] - field[:-1]) * (live_mask[1:] * live_mask[:-1])
    flux_out = change / (1.0 + change * change / (kappa * kappa))
    zero_row = jnp.zeros_like(flux_out[:1])
    return field + STEP_SIZE * (
        jnp.concatenate([flux_out, zero_row], 0) - jnp.concatenate([zero_row, flux_out], 0)
    )


def diffuse_steps(field, kappa, live_mask, step_count):
    for sweep_no in range(step_count):
        field = diffuse_once(field, kappa, live_mask)
    return field


def resample_rows(wire_signal, row_offsets, widths):
    depth_count = wire_signal.shape[0]
    block_rows = math.gcd(depth_count, 512)
    frame_index = jnp.arange(depth_count, dtype=jnp.int32)[None, None, :]
    weights = (1.0 / widths.astype(jnp.float32))[:, None, None]

    def one_block(first_depth):
        depth_index = first_depth + jnp.arange(block_rows, dtype=jnp.int32)[None, :, None]
        spacing = depth_index - frame_index - row_offsets[:, None, None]
        band_rows = jnp.where((spacing >= 0) & (spacing < widths[:, None, None]), weights, 0.0)
        return jnp.einsum("rdw,wrc->drc", band_rows, wire_signal, precision=lax.Precision.HIGHEST)

    starts = jnp.arange(depth_count // block_rows, dtype=jnp.int32) * block_rows
    pieces = lax.map(one_block, starts)
    return pieces.reshape(depth_count, wire_signal.shape[1], wire_signal.shape[2])


def body(frames, depth_offset, band_width, edge_level):
    local_frames = frames.shape[0]
    scan_count = lax.axis_size("scan")
    my_index = lax.axis_index("scan")
    all_frames = local_frames * scan_count
    rows_dev = frames.shape[1] // scan_count
    plane_rows = lax.all_to_all(frames, "scan", split_axis=1, concat_axis=0, tiled=True)
    full_mask = jnp.ones((all_frames, 1, 1), jnp.float32)
    plane_rows = diffuse_steps(plane_rows, TEMPORAL_KAPPA, full_mask, SWEEPS)
    wire_signal = jnp.concatenate(
        [plane_rows[:-1] - plane_rows[1:], jnp.zeros_like(plane_rows[:1])], 0
    )
    first_row = my_index * rows_dev
    row_offsets = lax.dynamic_slice_in_dim(depth_offset, first_row, rows_dev, 0)
    widths = lax.dynamic_slice_in_dim(band_width, first_row, rows_dev, 0)
    profile = resample_rows(wire_signal, row_offsets, widths)
    edge_scale = edge_level.astype(jnp.float32) / LEVEL_SCALE
    row_scale = lax.dynamic_slice_in_dim(edge_scale, first_row, rows_dev, 0)[None]
    full_mask = jnp.ones((all_frames, 1, 1), jnp.float32)
    profile = diffuse_steps(profile, row_scale, full_mask, DIFFUSE)
    return lax.all_to_all(profile, "scan", split_axis=0, concat_axis=1, tiled=True)


def solution(mesh):
    placed = (P("scan", None, "col"), P(), P(), P(None, "col"))
    return jax.shard_map(
        body, mesh=mesh, in_specs=placed, out_specs=P("scan", None, "col"), check_vma=False
    )
```

profile of v0, /device:TPU:64, one launch (start us, length us, event | category | flops | bytes accessed | tf_op | source)
XLA Modules:
  0.0 108.5 jit_solution(3032768076574771375)
XLA Ops:
  0.0 4.1 %copy.19 = f32[16,128,256]{2,0,1:T(8,128)} copy(f32[16,128,256]{2,1,0:T(8,128)} %param.4) | data formatting | bytes 4194304 | tf_op args[0]
  4.1 8.8 %all-to-all-start = ((f32[16,128,256]{2,0,1:T(8,128)}), f32[16,128,256]{2,0,1:T(8,128)S(1)}, u32[]{:S(2)}, u32[]{:S(2)}) async-start(f32[16,128,256]{2,0,1:T(8,128)} %copy.19), calls=%async_computation | async-start | bytes 4194304 | tf_op jit(solution)/shard_map/all_to_all | solution.py:55
  13.1 0.7 fusion.17
  14.0 31.1 %all-to-all-done = f32[16,128,256]{2,0,1:T(8,128)S(1)} async-done(((f32[16,128,256]{2,0,1:T(8,128)}), f32[16,128,256]{2,0,1:T(8,128)S(1)}, u32[]{:S(2)}, u32[]{:S(2)}) %all-to-all-start) | async-done | bytes 2097184 | tf_op jit(solution)/shard_map/all_to_all | solution.py:55
  45.0 1.5 %copy.20 = f32[32,16,4,256]{3,1,0,2:T(8,128)} copy(f32[32,16,4,256]{3,1,2,0:T(8,128)S(1)} %bitcast.10) | data formatting | bytes 4194304 | tf_op jit(solution)/shard_map/all_to_all | solution.py:55
  46.6 2.1 %copy.23 = f32[512,4,256]{0,2,1:T(8,128)S(1)} copy(f32[512,4,256]{2,0,1:T(8,128)} %bitcast.11) | data formatting | bytes 4194304 | tf_op jit(solution)/shard_map/all_to_all | solution.py:55
  48.7 0.6 add_divide_fusion.11
  49.3 0.8 multiply_add_fusion.11
  50.1 0.6 add_divide_fusion.10
  50.7 0.8 multiply_add_fusion.10
  52.2 0.8 multiply_add_fusion.9
  53.6 0.8 multiply_add_fusion.8
  54.4 0.6 add_divide_fusion.7
  55.1 0.8 multiply_add_fusion.7
  55.9 0.6 add_divide_fusion.6
  56.5 0.8 multiply_add_fusion.6
  57.9 4.6 %fusion.11 = f32[512,4,256]{0,2,1:T(8,128)S(1)} fusion(f32[4]{0:T(128)S(1)} %get-tuple-element.17, s32[4]{0:T(128)S(1)} %get-tuple-element.18, s32[4]{0:T(128)S(1)} %dynamic_slice.12, s32[512,512]{1,0:T(8,128)S(1)} %iota_subtract_fusion, f32[511,4,256]{0,2,1:T(8,128)S(1)} %slice_subtract_fusion.6), kind=kOutput, calls=%fused_computation.49 | convolution fusion | flops 3226468352 | bytes 5238832 | tf_op jit(solution)/shard_map/while/body/eval_jaxpr/rdw,wrc->drc/dot_general | solution.py:42
  62.5 0.8 add_divide_fusion.5
  63.3 0.8 multiply_add_fusion.5
  64.1 0.8 add_divide_fusion.4
  64.9 0.8 multiply_add_fusion.4
  65.8 0.8 add_divide_fusion.3
  66.5 0.8 multiply_add_fusion.3
  67.4 0.8 add_divide_fusion.2
  68.2 0.8 multiply_add_fusion.2
  69.0 0.8 add_divide_fusion.1
  69.8 0.8 multiply_add_fusion.1
  70.6 0.8 add_divide_fusion
  71.4 0.8 multiply_add_fusion
  72.2 1.8 %copy.24 = f32[512,4,256]{2,1,0:T(4,128)} copy(f32[512,4,256]{0,2,1:T(8,128)S(1)} %multiply_add_fusion) | data formatting | bytes 4194304 | tf_op jit(solution)/shard_map/add | solution.py:21
  74.0 31.3 %all_to_all.36 = f32[512,4,256]{2,1,0:T(4,128)S(1)} all-to-all(f32[512,4,256]{2,1,0:T(4,128)} %copy.24), channel_id=1, replica_groups=mesh['scan'=32,'col'=8] {'scan'}, dimensions={0} | all-to-all | bytes 4194304 | tf_op jit(solution)/shard_map/all_to_all | solution.py:69
  106.0 2.5 %copy.27 = f32[16,128,256]{2,1,0:T(8,128)} copy(f32[16,128,256]{2,0,1:T(8,128)S(1)} %bitcast.13) | data formatting | bytes 4194304 | tf_op jit(solution)/shard_map/all_to_all | solution.py:69
  (12 shorter events, 2.8 us)
Async XLA Ops:
  4.1 8.8 %copy-start.1 = (s32[128]{0:T(128)S(1)}, s32[128]{0:T(128)}, u32[]{:S(2)}) copy-start(s32[128]{0:T(128)} %param.5) | copy-start | bytes 1540
  4.1 8.9 %copy-start = (s32[128]{0:T(128)S(1)}, s32[128]{0:T(128)}, u32[]{:S(2)}) copy-start(s32[128]{0:T(128)} %param.6) | copy-start | bytes 1540
  4.1 40.9 %all-to-all-start = ((f32[16,128,256]{2,0,1:T(8,128)}), f32[16,128,256]{2,0,1:T(8,128)S(1)}, u32[]{:S(2)}, u32[]{:S(2)}) async-start(f32[16,128,256]{2,0,1:T(8,128)} %copy.19), calls=%async_computation | async-start | bytes 4194304 | tf_op jit(solution)/shard_map/all_to_all | solution.py:55
where the time goes:
time: 109 us
  blocking collectives  31.3 us (29%)
  waiting for transfers between devices  31.1 us (29%)
  other arithmetic  19.6 us (18%)
  local copies, waits for them, and re-layouts  12.8 us (12%)
  starting transfers between devices  8.81 us (8%)
  matrix products  4.59 us (4%)
    all_to_all x1, blocking collectives, body(): lax.all_to_all(profile, 'scan', split_axis=0, concat_axis=1, tiled=True)  31.3 us
    all_to_all x1, waiting for transfers between devices, body(): lax.all_to_all(frames, 'scan', split_axis=1, concat_axis=0, tiled=True)  31.1 us
    add x12, other arithmetic, diffuse_once(): field + STEP_SIZE * (jnp.concatenate([flux_out, zero_row], 0) - jnp.conca...  9.69 us
    all_to_all x1, starting transfers between devices, body(): lax.all_to_all(frames, 'scan', split_axis=1, concat_axis=0, tiled=True)  8.81 us
    div x12, other arithmetic, diffuse_once(): flux_out = change / (1.0 + change * change / (kappa * kappa))  8.43 us
    dot_general x1, matrix products, one_block(): jnp.einsum('rdw,wrc->drc', band_rows, wire_signal, precision=lax.Precisio...  4.59 us
    unnamed x5, local copies, waits for them, and re-layouts  4.13 us
    all_to_all x2, local copies, waits for them, and re-layouts, body(): lax.all_to_all(frames, 'scan', split_axis=1, concat_axis=0, tiled=True)  3.64 us
  transfers between devices with their start and end apart: 1, of which 1 were waited for; matrix products, arithmetic and copies ran while one was open for 1% of the time, Pallas kernels for 0%

commit v1 on v0

v1 whole, which is shorter than its diff:
```python
import functools
import math

import jax
import jax.numpy as jnp
from jax import lax
from jax.experimental import pallas as pl
from jax.experimental.pallas import tpu as pltpu
from jax.sharding import PartitionSpec as P

SWEEPS = 6
DIFFUSE = 6
TEMPORAL_KAPPA = 1.0
STEP_SIZE = 0.24
LEVEL_SCALE = 16.0
BAND = 8
SHIFT = 128
SUB = 8
LANES = 128

INV_STEP = 1.0 / STEP_SIZE
ROOT_STEP = math.sqrt(STEP_SIZE)
LOW_PAD = SHIFT + BAND
HIGH_PAD = SHIFT + BAND


def sweep(count, load, store):
    here = load(0)
    flux_in = None
    for i in range(count):
        if i < count - 1:
            ahead = load(i + 1)
            change = ahead - here
            flux_out = change / (INV_STEP + change * change)
            store(i, here + (flux_out if flux_in is None else flux_out - flux_in))
            flux_in, here = flux_out, ahead
        else:
            store(i, here - flux_in)


def lines_kernel(count, offset_ref, width_ref, level_ref, lines_ref, out_ref, padded_ref):
    scale_in = 1.0 / (TEMPORAL_KAPPA * ROOT_STEP)

    def put(i, value):
        padded_ref[LOW_PAD + i] = value

    def get(i):
        return padded_ref[LOW_PAD + i]

    sweep(count, lambda i: lines_ref[i] * scale_in, put)

    def again(_, carry):
        sweep(count, get, put)
        return carry

    lax.fori_loop(0, SWEEPS - 1, again, 0)

    first, last = get(0), get(count - 1)
    for i in range(LOW_PAD):
        padded_ref[i] = first
    for i in range(HIGH_PAD):
        padded_ref[LOW_PAD + count + i] = last

    sublane = lax.broadcasted_iota(jnp.int32, (SUB, LANES), 0)
    width = jnp.zeros((SUB, LANES), jnp.int32)
    starts = []
    for r in range(SUB):
        starts.append(LOW_PAD + 1 - offset_ref[r] - width_ref[r])
        width = jnp.where(sublane == r, width_ref[r], width)
    level = level_ref[...].astype(jnp.float32)
    gain = LEVEL_SCALE / (width.astype(jnp.float32) * level)
    rows = [sublane == r for r in range(SUB)]
    less = width - 1
    bits = [(less & 1) != 0, (less & 2) != 0, (less & 4) != 0]

    def shifted(i):
        value = padded_ref[starts[0] + i]
        for r in range(1, SUB):
            value = jnp.where(rows[r], padded_ref[starts[r] + i], value)
        return value

    window = [shifted(i) for i in range(BAND + 1)]
    ones = [jnp.where(bits[0], window[i + 2], window[i + 1]) for i in range(BAND - 1)]
    twos = [jnp.where(bits[1], ones[i + 2], ones[i]) for i in range(BAND - 3)]
    for d in range(count):
        if d:
            window = window[1:] + [shifted(d + BAND)]
            ones = ones[1:] + [jnp.where(bits[0], window[BAND], window[BAND - 1])]
            twos = twos[1:] + [jnp.where(bits[1], ones[BAND - 2], ones[BAND - 4])]
        out_ref[d] = (window[0] - jnp.where(bits[2], twos[4], twos[0])) * gain

    def out_put(i, value):
        out_ref[i] = value

    def out_again(_, carry):
        sweep(count, lambda i: out_ref[i], out_put)
        return carry

    lax.fori_loop(0, DIFFUSE - 1, out_again, 0)
    scale_out = level * (ROOT_STEP / LEVEL_SCALE)

    def out_final(i, value):
        out_ref[i] = value * scale_out

    sweep(count, lambda i: out_ref[i], out_final)


def process_lines(lines, offsets, widths, levels):
    count = lines.shape[0]
    smem = pl.BlockSpec(memory_space=pltpu.SMEM)
    vmem = pl.BlockSpec(memory_space=pltpu.VMEM)
    return pl.pallas_call(
        functools.partial(lines_kernel, count),
        out_shape=jax.ShapeDtypeStruct(lines.shape, jnp.float32),
        in_specs=[smem, smem, vmem, vmem],
        out_specs=vmem,
        scratch_shapes=[pltpu.VMEM((LOW_PAD + count + HIGH_PAD, SUB, LANES), jnp.float32)],
        compiler_params=pltpu.CompilerParams(vmem_limit_bytes=12 << 20),
        name="lines",
    )(offsets, widths, levels, lines)


def body(frames, depth_offset, band_width, edge_level):
    scan_count = lax.axis_size("scan")
    me = lax.axis_index("scan")
    held, rows, cols = frames.shape
    groups, halves = rows // SUB, cols // LANES
    assert groups * halves == scan_count
    tiles = frames.reshape(held, groups, SUB, halves, LANES).transpose(1, 3, 0, 2, 4)
    tiles = tiles.reshape(scan_count, held, SUB, LANES)
    lines = lax.all_to_all(tiles, "scan", split_axis=0, concat_axis=0, tiled=True)
    lines = lines.reshape(scan_count * held, SUB, LANES)
    first_row = (me // halves) * SUB
    offsets = lax.dynamic_slice_in_dim(depth_offset, first_row, SUB, 0)
    widths = lax.dynamic_slice_in_dim(band_width, first_row, SUB, 0)
    levels = lax.dynamic_slice(edge_level, (first_row, (me % halves) * LANES), (SUB, LANES))
    done = process_lines(lines, offsets, widths, levels)
    done = done.reshape(scan_count, held, SUB, LANES)
    back = lax.all_to_all(done, "scan", split_axis=0, concat_axis=0, tiled=True)
    back = back.reshape(groups, halves, held, SUB, LANES).transpose(2, 0, 3, 1, 4)
    return back.reshape(held, rows, cols)


def solution(mesh):
    placed = (P("scan", None, "col"), P(), P(), P(None, "col"))
    return jax.shard_map(
        body, mesh=mesh, in_specs=placed, out_specs=P("scan", None, "col"), check_vma=False
    )
```

time: 109 us -> 84 us (0.77)
  other arithmetic: 19.6 us -> 0 us
  Pallas kernels: 0 us -> 7.89 us
  local copies, waits for them, and re-layouts: 12.8 us -> 5.54 us
  matrix products: 4.59 us -> 0 us
    add x12 -> x0, other arithmetic: 9.69 us -> none  [diffuse_once(): field + STEP_SIZE * (jnp.concatenate([flux_out, zero_row], 0) - jnp.conca...]
    div x13 -> x0, other arithmetic: 8.5 us -> none  [the longest x12 8.43 us: diffuse_once(): flux_out = change / (1.0 + change * change / (kappa * kappa))]
    pallas_call x0 -> x1, Pallas kernels: none -> 7.89 us  [process_lines(): pl.pallas_call(functools.partial(lines_kernel, count), out_shape=jax.Shap...]
    all_to_all x5 -> x0, local copies, waits for them, and re-layouts: 6.82 us -> none  [the longest x2 3.64 us: body(): lax.all_to_all(frames, 'scan', split_axis=1, concat_axis=0, tiled=True)]
    dot_general x1 -> x0, matrix products: 4.59 us -> none  [one_block(): jnp.einsum('rdw,wrc->drc', band_rows, wire_signal, precision=lax.Precisio...]
    unnamed x5 -> x4, local copies, waits for them, and re-layouts: 4.13 us -> 0.01 us
    transpose x0 -> x1, local copies, waits for them, and re-layouts: none -> 3.17 us  [body(): frames.reshape(held, groups, SUB, halves, LANES).transpose(1, 3, 0, 2, 4)]
    add x1 -> x0, local copies, waits for them, and re-layouts: 1.81 us -> none  [diffuse_once(): field + STEP_SIZE * (jnp.concatenate([flux_out, zero_row], 0) - jnp.conca...]
where the time goes in v1:
time: 84 us; the launch traced here: 83.8 us
  waiting for transfers between devices  31.2 us (37%)
  blocking collectives  30.3 us (36%)
  starting transfers between devices  8.81 us (10%)
  Pallas kernels  7.89 us (9%)
  local copies, waits for them, and re-layouts  5.54 us (7%)
    all_to_all x1, waiting for transfers between devices, body(): lax.all_to_all(tiles, 'scan', split_axis=0, concat_axis=0, tiled=True)  31.2 us
    all_to_all x1, blocking collectives, body(): back = lax.all_to_all(done, 'scan', split_axis=0, concat_axis=0, tiled=True)  30.3 us
    all_to_all x1, starting transfers between devices, body(): lax.all_to_all(tiles, 'scan', split_axis=0, concat_axis=0, tiled=True)  8.81 us
    pallas_call x1, Pallas kernels, process_lines(): pl.pallas_call(functools.partial(lines_kernel, count), out_shape=jax.Shap...  7.89 us
    transpose x1, local copies, waits for them, and re-layouts, body(): frames.reshape(held, groups, SUB, halves, LANES).transpose(1, 3, 0, 2, 4)  3.17 us
  transfers between devices with their start and end apart: 1, of which 1 were waited for; matrix products, arithmetic and copies ran while one was open for 1% of the time, Pallas kernels for 0%

profile of v1, /device:TPU:64, one launch (start us, length us, event | category | flops | bytes accessed | tf_op | source)
XLA Modules:
  0.0 83.8 jit_solution(10514891498858471141)
XLA Ops:
  0.0 3.2 %copy.5 = f32[16,2,16,8,128]{4,3,2,1,0:T(8,128)} copy(f32[16,2,16,8,128]{4,3,1,0,2:T(8,128)} %bitcast.16) | data formatting | bytes 4194304 | tf_op jit(solution)/shard_map/transpose | solution.py:129
  3.2 0.0 copy-start
  3.2 0.0 copy-start.1
  3.2 8.8 %all-to-all-start = ((f32[32,16,8,128]{3,2,1,0:T(8,128)}), f32[32,16,8,128]{3,2,1,0:T(8,128)S(1)}, u32[]{:S(2)}, u32[]{:S(2)}) async-start(f32[32,16,8,128]{3,2,1,0:T(8,128)} %bitcast.14), calls=%async_computation | async-start | bytes 4194304 | tf_op jit(solution)/shard_map/all_to_all | solution.py:131
  12.0 0.0 copy-done
  12.0 0.1 dynamic_slice.9.offset_ref
  12.1 0.0 copy-done.1
  12.1 0.1 dynamic_slice.10.width_ref
  12.2 0.7 dynamic_slice.11.level_ref
  12.9 31.2 %all-to-all-done = f32[32,16,8,128]{3,2,1,0:T(8,128)S(1)} async-done(((f32[32,16,8,128]{3,2,1,0:T(8,128)}), f32[32,16,8,128]{3,2,1,0:T(8,128)S(1)}, u32[]{:S(2)}, u32[]{:S(2)}) %all-to-all-start) | async-done | bytes 2097184 | tf_op jit(solution)/shard_map/all_to_all | solution.py:131
  44.1 7.9 %lines.1 = f32[512,8,128]{2,1,0:T(8,128)S(1)} custom-call(s32[8]{0:T(128)S(1)} %dynamic_slice.9.offset_ref, s32[8]{0:T(128)S(1)} %dynamic_slice.10.width_ref, s32[8,128]{1,0:T(8,128)S(1)} %dynamic_slice.11.level_ref, f32[512,8,128]{2,1,0:T(8,128)S(1)} %bitcast.12), custom_call_target="tpu_custom_call" | custom-call | tf_op jit(solution)/shard_map/lines/pallas_call | solution.py:112
  52.0 30.3 %all_to_all.10 = f32[32,16,8,128]{3,2,1,0:T(8,128)S(1)} all-to-all(f32[32,16,8,128]{3,2,1,0:T(8,128)S(1)} %bitcast.13), channel_id=1, replica_groups=mesh['scan'=32,'col'=8] {'scan'}, dimensions={0} | all-to-all | bytes 4194304 | tf_op jit(solution)/shard_map/all_to_all | solution.py:139
  82.3 1.5 %copy.8 = f32[16,2,16,8,128]{4,3,1,0,2:T(8,128)} copy(f32[16,2,16,8,128]{4,3,2,1,0:T(8,128)S(1)} %bitcast.15) | data formatting | bytes 4194304 | tf_op jit(solution)/shard_map/reshape | solution.py:140
Async XLA Ops:
  3.2 8.8 %copy-start = (s32[128]{0:T(128)S(1)}, s32[128]{0:T(128)}, u32[]{:S(2)}) copy-start(s32[128]{0:T(128)} %param.5) | copy-start | bytes 1540
  3.2 8.9 %copy-start.1 = (s32[128]{0:T(128)S(1)}, s32[128]{0:T(128)}, u32[]{:S(2)}) copy-start(s32[128]{0:T(128)} %param.6) | copy-start | bytes 1540
  3.2 40.9 %all-to-all-start = ((f32[32,16,8,128]{3,2,1,0:T(8,128)}), f32[32,16,8,128]{3,2,1,0:T(8,128)S(1)}, u32[]{:S(2)}, u32[]{:S(2)}) async-start(f32[32,16,8,128]{3,2,1,0:T(8,128)} %bitcast.14), calls=%async_computation | async-start | bytes 4194304 | tf_op jit(solution)/shard_map/all_to_all | solution.py:131

commit v2 on v1

--- a/solution.py
+++ b/solution.py
@@ -17,6 +17,7 @@
 SHIFT = 128
 SUB = 8
 LANES = 128
+HANDOVERS = 2
 
 INV_STEP = 1.0 / STEP_SIZE
 ROOT_STEP = math.sqrt(STEP_SIZE)
@@ -38,7 +39,23 @@
             store(i, here - flux_in)
 
 
-def lines_kernel(count, offset_ref, width_ref, level_ref, lines_ref, out_ref, padded_ref):
+def lines_kernel(
+    count, offset_hbm, width_hbm, level_hbm, lines_ref, out_ref,
+    padded_ref, offset_ref, width_ref, level_ref, sems,
+):
+    halves = level_hbm.shape[1] // LANES
+    me = lax.axis_index("scan")
+    base = pl.multiple_of((me // halves) * SUB, SUB)
+    column = pl.multiple_of((me % halves) * LANES, LANES)
+    fetches = [
+        pltpu.make_async_copy(offset_hbm, offset_ref, sems.at[0]),
+        pltpu.make_async_copy(width_hbm, width_ref, sems.at[1]),
+        pltpu.make_async_copy(
+            level_hbm.at[pl.ds(base, SUB), pl.ds(column, LANES)], level_ref, sems.at[2]
+        ),
+    ]
+    for fetch in fetches:
+        fetch.start()
     scale_in = 1.0 / (TEMPORAL_KAPPA * ROOT_STEP)
 
     def put(i, value):
@@ -61,12 +78,14 @@
     for i in range(HIGH_PAD):
         padded_ref[LOW_PAD + count + i] = last
 
+    for fetch in fetches:
+        fetch.wait()
     sublane = lax.broadcasted_iota(jnp.int32, (SUB, LANES), 0)
     width = jnp.zeros((SUB, LANES), jnp.int32)
     starts = []
     for r in range(SUB):
-        starts.append(LOW_PAD + 1 - offset_ref[r] - width_ref[r])
-        width = jnp.where(sublane == r, width_ref[r], width)
+        starts.append(LOW_PAD + 1 - offset_ref[base + r] - width_ref[base + r])
+        width = jnp.where(sublane == r, width_ref[base + r], width)
     level = level_ref[...].astype(jnp.float32)
     gain = LEVEL_SCALE / (width.astype(jnp.float32) * level)
     rows = [sublane == r for r in range(SUB)]
@@ -105,39 +124,55 @@
     sweep(count, lambda i: out_ref[i], out_final)
 
 
-def process_lines(lines, offsets, widths, levels):
+def process_lines(lines, depth_offset, band_width, edge_level):
     count = lines.shape[0]
-    smem = pl.BlockSpec(memory_space=pltpu.SMEM)
     vmem = pl.BlockSpec(memory_space=pltpu.VMEM)
+    hbm = pl.BlockSpec(memory_space=pltpu.HBM)
     return pl.pallas_call(
         functools.partial(lines_kernel, count),
         out_shape=jax.ShapeDtypeStruct(lines.shape, jnp.float32),
-        in_specs=[smem, smem, vmem, vmem],
+        in_specs=[hbm, hbm, hbm, vmem],
         out_specs=vmem,
-        scratch_shapes=[pltpu.VMEM((LOW_PAD + count + HIGH_PAD, SUB, LANES), jnp.float32)],
+        scratch_shapes=[
+            pltpu.VMEM((LOW_PAD + count + HIGH_PAD, SUB, LANES), jnp.float32),
+            pltpu.SMEM(depth_offset.shape, jnp.int32),
+            pltpu.SMEM(band_width.shape, jnp.int32),
+            pltpu.VMEM((SUB, LANES), jnp.int32),
+            pltpu.SemaphoreType.DMA((3,)),
+        ],
         compiler_params=pltpu.CompilerParams(vmem_limit_bytes=12 << 20),
         name="lines",
-    )(offsets, widths, levels, lines)
+    )(depth_offset, band_width, edge_level, lines)
 
 
 def body(frames, depth_offset, band_width, edge_level):
     scan_count = lax.axis_size("scan")
-    me = lax.axis_index("scan")
     held, rows, cols = frames.shape
     groups, halves = rows // SUB, cols // LANES
     assert groups * halves == scan_count
-    tiles = frames.reshape(held, groups, SUB, halves, LANES).transpose(1, 3, 0, 2, 4)
-    tiles = tiles.reshape(scan_count, held, SUB, LANES)
-    lines = lax.all_to_all(tiles, "scan", split_axis=0, concat_axis=0, tiled=True)
+
+    def tiled(part):
+        tiles = part.reshape(held, groups, SUB, halves, LANES).transpose(1, 3, 0, 2, 4)
+        return tiles.reshape(scan_count, held, SUB, LANES)
+
+    def exchange(tiles):
+        return lax.all_to_all(tiles, "scan", split_axis=0, concat_axis=0, tiled=True)
+
+    def after_token(frames):
+        pairs = [(p, p ^ 1) for p in range(scan_count)]
+        token = frames[0, :SUB, :LANES]
+        for _ in range(HANDOVERS):
+            token = lax.ppermute(token, "scan", pairs)
+        return exchange(tiled(frames) + 0.0 * token[0, 0])
+
+    def at_once(frames):
+        return exchange(tiled(frames))
+
+    lines = lax.cond(lax.axis_index("col") % 2 == 0, after_token, at_once, frames)
     lines = lines.reshape(scan_count * held, SUB, LANES)
-    first_row = (me // halves) * SUB
-    offsets = lax.dynamic_slice_in_dim(depth_offset, first_row, SUB, 0)
-    widths = lax.dynamic_slice_in_dim(band_width, first_row, SUB, 0)
-    levels = lax.dynamic_slice(edge_level, (first_row, (me % halves) * LANES), (SUB, LANES))
-    done = process_lines(lines, offsets, widths, levels)
-    done = done.reshape(scan_count, held, SUB, LANES)
-    back = lax.all_to_all(done, "scan", split_axis=0, concat_axis=0, tiled=True)
-    back = back.reshape(groups, halves, held, SUB, LANES).transpose(2, 0, 3, 1, 4)
+    done = process_lines(lines, depth_offset, band_width, edge_level)
+    back = lax.all_to_all(done.reshape(scan_count * held, 1, SUB, LANES), "scan", split_axis=0, concat_axis=1, tiled=True)
+    back = back.reshape(held, groups, halves, SUB, LANES).transpose(0, 1, 3, 2, 4)
     return back.reshape(held, rows, cols)
 
 

time: 84 us -> 72.2 us (0.86)
  waiting for transfers between devices: 31.2 us -> 3.38 us
  blocking collectives: 30.3 us -> 51.9 us
  starting transfers between devices: 8.81 us -> 3.83 us
  local copies, waits for them, and re-layouts: 5.54 us -> 3.05 us
  other arithmetic: 0 us -> 1.74 us
    all_to_all x1 -> x0, waiting for transfers between devices: 31.2 us -> none  [body(): lax.all_to_all(tiles, 'scan', split_axis=0, concat_axis=0, tiled=True)]
    all_to_all x1 -> x2, blocking collectives: 30.3 us -> 51.9 us  [the longest x1 28.4 us: exchange(): lax.all_to_all(tiles, 'scan', split_axis=0, concat_axis=0, tiled=True)]
    all_to_all x1 -> x0, starting transfers between devices: 8.81 us -> none  [body(): lax.all_to_all(tiles, 'scan', split_axis=0, concat_axis=0, tiled=True)]
    ppermute x0 -> x2, starting transfers between devices: none -> 3.83 us  [after_token(): token = lax.ppermute(token, 'scan', pairs)]
    ppermute x0 -> x2, waiting for transfers between devices: none -> 3.38 us  [after_token(): token = lax.ppermute(token, 'scan', pairs)]
    transpose x1 -> x0, local copies, waits for them, and re-layouts: 3.17 us -> none  [body(): frames.reshape(held, groups, SUB, halves, LANES).transpose(1, 3, 0, 2, 4)]
    add x0 -> x1, other arithmetic: none -> 1.74 us  [after_token(): return exchange(tiled(frames) + 0.0 * token[0, 0])]
  transfers between devices with their start and end apart: 1 -> 2, of which waited for: 1 -> 2; matrix products, arithmetic and copies ran while one was open for 1% -> 0% of each run, Pallas kernels for 0% -> 0%
where the time goes in v2:
time: 72.2 us; the launch traced here: 72.3 us
  blocking collectives  51.9 us (72%)
  Pallas kernels  7.7 us (11%)
  starting transfers between devices  3.83 us (5%)
  waiting for transfers between devices  3.38 us (5%)
  local copies, waits for them, and re-layouts  3.05 us (4%)
  other arithmetic  1.74 us (2%)
    all_to_all x1, blocking collectives, exchange(): lax.all_to_all(tiles, 'scan', split_axis=0, concat_axis=0, tiled=True)  28.4 us
    all_to_all x1, blocking collectives, body(): lax.all_to_all(done.reshape(scan_count * held, 1, SUB, LANES), 'scan', sp...  23.6 us
    pallas_call x1, Pallas kernels, process_lines(): pl.pallas_call(functools.partial(lines_kernel, count), out_shape=jax.Shap...  7.7 us
    ppermute x2, starting transfers between devices, after_token(): token = lax.ppermute(token, 'scan', pairs)  3.83 us
    ppermute x2, waiting for transfers between devices, after_token(): token = lax.ppermute(token, 'scan', pairs)  3.38 us
    add x1, other arithmetic, after_token(): return exchange(tiled(frames) + 0.0 * token[0, 0])  1.74 us
    reshape x1, local copies, waits for them, and re-layouts, body(): back.reshape(held, groups, halves, SUB, LANES).transpose(0, 1, 3, 2, 4)  1.53 us
  transfers between devices with their start and end apart: 2, of which 2 were waited for; matrix products, arithmetic and copies ran while one was open for 0% of the time, Pallas kernels for 0%

profile of v2, /device:TPU:64, one launch (start us, length us, event | category | flops | bytes accessed | tf_op | source)
XLA Modules:
  0.0 72.3 jit_solution(6107283192367512807)
XLA Ops:
  0.0 0.0 copy-start
  0.0 0.0 copy-start.1
  0.0 0.0 copy-start.2
  0.0 39.4 %conditional.1 = (f32[512,8,128]{2,1,0:T(8,128)S(1)}) conditional(s32[]{:T(128)} %convert_element_type.3, f32[16,128,256]{2,1,0:T(8,128)} %param.6, f32[16,128,256]{2,1,0:T(8,128)} %param.6), branch_computations={%region_0.1_spmd, %region_1.2_spmd} | conditional | flops 524289 | bytes 12623984 | solution.py:171
  0.0 0.8 %slice_bitcast_fusion = f32[8,128]{1,0:T(8,128)S(1)} fusion(f32[16,128,256]{2,1,0:T(8,128)} %param.1), kind=kLoop, calls=%fused_computation.1 | loop fusion | bytes 8192 | tf_op jit(solution)/shard_map/cond/branch_1_fun/squeeze | solution.py:163
  0.8 1.9 %collective-permute-start = (f32[8,128]{1,0:T(8,128)S(1)}, f32[8,128]{1,0:T(8,128)S(1)}, u32[]{:S(2)}, u32[]{:S(2)}) collective-permute-start(f32[8,128]{1,0:T(8,128)S(1)} %slice_bitcast_fusion), channel_id=1, source_target_pairs={{0,8},{8,0},{16,24},{24,16},{32,40},{40,32},{48,56},{56,48},{64,72... | collective-permute-start | bytes 12296 | tf_op jit(solution)/shard_map/cond/branch_1_fun/ppermute | solution.py:165
  2.7 1.7 %collective-permute-done = f32[8,128]{1,0:T(8,128)S(1)} collective-permute-done((f32[8,128]{1,0:T(8,128)S(1)}, f32[8,128]{1,0:T(8,128)S(1)}, u32[]{:S(2)}, u32[]{:S(2)}) %collective-permute-start) | collective-permute-done | bytes 4128 | tf_op jit(solution)/shard_map/cond/branch_1_fun/ppermute | solution.py:165
  4.4 1.9 %collective-permute-start.1 = (f32[8,128]{1,0:T(8,128)S(1)}, f32[8,128]{1,0:T(8,128)S(1)}, u32[]{:S(2)}, u32[]{:S(2)}) collective-permute-start(f32[8,128]{1,0:T(8,128)S(1)} %collective-permute-done), channel_id=1, source_target_pairs={{0,8},{8,0},{16,24},{24,16},{32,40},{40,32},{48,56},{56,48},{64,72... | collective-permute-start | bytes 12296 | tf_op jit(solution)/shard_map/cond/branch_1_fun/ppermute | solution.py:165
  6.3 1.7 %collective-permute-done.1 = f32[8,128]{1,0:T(8,128)S(1)} collective-permute-done((f32[8,128]{1,0:T(8,128)S(1)}, f32[8,128]{1,0:T(8,128)S(1)}, u32[]{:S(2)}, u32[]{:S(2)}) %collective-permute-start.1) | collective-permute-done | bytes 4128 | tf_op jit(solution)/shard_map/cond/branch_1_fun/ppermute | solution.py:165
  8.0 0.5 slice.5
  9.1 1.7 %add_bitcast_fusion = f32[16,2,16,8,128]{4,3,1,0,2:T(8,128)S(1)} fusion(f32[16,128,256]{2,1,0:T(8,128)} %param.1, f32[]{:T(128)} %bitcast.6), kind=kLoop, calls=%fused_computation | loop fusion | flops 524288 | bytes 4194308 | tf_op jit(solution)/shard_map/cond/branch_1_fun/add | solution.py:166
  10.8 0.2 copy.9
  11.1 28.4 %all_to_all.24 = f32[32,16,8,128]{3,2,1,0:T(8,128)S(1)} all-to-all(f32[32,16,8,128]{3,2,1,0:T(8,128)S(1)} %bitcast.31), channel_id=1, replica_groups=mesh['scan'=32,'col'=8] {'scan'}, dimensions={0} | all-to-all | bytes 4194304 | tf_op jit(solution)/shard_map/cond/branch_1_fun/all_to_all | solution.py:159
  39.4 0.0 copy-done
  39.5 0.0 copy-done.1
  39.5 0.0 copy-done.2
  39.5 7.7 %lines.1 = f32[512,8,128]{2,1,0:T(8,128)S(1)} custom-call(s32[128]{0:T(128)S(1)} %copy-done.1, s32[128]{0:T(128)S(1)} %copy-done.2, s32[128,256]{1,0:T(8,128)S(1)} %copy-done, f32[512,8,128]{2,1,0:T(8,128)S(1)} %get-tuple-element.11.lines_ref), custom_call_target="tpu_custom_call" | custom-call | tf_op jit(solution)/shard_map/lines/pallas_call | solution.py:131
  47.2 23.6 %all_to_all.25 = f32[512,1,8,128]{3,2,1,0:T(8,128)S(1)} all-to-all(f32[512,1,8,128]{3,2,1,0:T(8,128)S(1)} %bitcast.27), channel_id=1, replica_groups=mesh['scan'=32,'col'=8] {'scan'}, dimensions={0} | all-to-all | bytes 4194304 | tf_op jit(solution)/shard_map/all_to_all | solution.py:174
  70.7 1.5 %copy.13 = f32[16,16,2,8,128]{4,3,2,1,0:T(8,128)} copy(f32[16,16,2,8,128]{4,3,0,2,1:T(8,128)S(1)} %bitcast.32) | data formatting | bytes 4194304 | tf_op jit(solution)/shard_map/reshape | solution.py:175
Async XLA Ops:
  0.0 39.4 %copy-start = (s32[128,256]{1,0:T(8,128)S(1)}, s32[128,256]{1,0:T(8,128)}, u32[]{:S(2)}) copy-start(s32[128,256]{1,0:T(8,128)} %level_hbm.1) | copy-start | bytes 393220
  0.0 39.4 %copy-start.1 = (s32[128]{0:T(128)S(1)}, s32[128]{0:T(128)}, u32[]{:S(2)}) copy-start(s32[128]{0:T(128)} %offset_hbm.1) | copy-start | bytes 1540
  0.0 39.5 %copy-start.2 = (s32[128]{0:T(128)S(1)}, s32[128]{0:T(128)}, u32[]{:S(2)}) copy-start(s32[128]{0:T(128)} %width_hbm.1) | copy-start | bytes 1540
  0.8 3.6 %collective-permute-start = (f32[8,128]{1,0:T(8,128)S(1)}, f32[8,128]{1,0:T(8,128)S(1)}, u32[]{:S(2)}, u32[]{:S(2)}) collective-permute-start(f32[8,128]{1,0:T(8,128)S(1)} %slice_bitcast_fusion), channel_id=1, source_target_pairs={{0,8},{8,0},{16,24},{24,16},{32,40},{40,32},{48,56},{56,48},{64,72... | collective-permute-start | bytes 12296 | tf_op jit(solution)/shard_map/cond/branch_1_fun/ppermute | solution.py:165
  4.4 3.6 %collective-permute-start.1 = (f32[8,128]{1,0:T(8,128)S(1)}, f32[8,128]{1,0:T(8,128)S(1)}, u32[]{:S(2)}, u32[]{:S(2)}) collective-permute-start(f32[8,128]{1,0:T(8,128)S(1)} %collective-permute-done), channel_id=1, source_target_pairs={{0,8},{8,0},{16,24},{24,16},{32,40},{40,32},{48,56},{56,48},{64,72... | collective-permute-start | bytes 12296 | tf_op jit(solution)/shard_map/cond/branch_1_fun/ppermute | solution.py:165

commit v3 on v2

--- a/solution.py
+++ b/solution.py
@@ -41,7 +41,7 @@
 
 def lines_kernel(
     count, offset_hbm, width_hbm, level_hbm, lines_ref, out_ref,
-    padded_ref, offset_ref, width_ref, level_ref, sems,
+    padded_ref, shifted_ref, offset_ref, width_ref, level_ref, sems,
 ):
     halves = level_hbm.shape[1] // LANES
     me = lax.axis_index("scan")
@@ -59,10 +59,10 @@
     scale_in = 1.0 / (TEMPORAL_KAPPA * ROOT_STEP)
 
     def put(i, value):
-        padded_ref[LOW_PAD + i] = value
+        padded_ref[pl.ds(SUB * (LOW_PAD + i), SUB), :] = value
 
     def get(i):
-        return padded_ref[LOW_PAD + i]
+        return padded_ref[pl.ds(SUB * (LOW_PAD + i), SUB), :]
 
     sweep(count, lambda i: lines_ref[i] * scale_in, put)
 
@@ -70,13 +70,20 @@
         sweep(count, get, put)
         return carry
 
-    lax.fori_loop(0, SWEEPS - 1, again, 0)
-
-    first, last = get(0), get(count - 1)
-    for i in range(LOW_PAD):
-        padded_ref[i] = first
-    for i in range(HIGH_PAD):
-        padded_ref[LOW_PAD + count + i] = last
+    lax.fori_loop(0, SWEEPS - 2, again, 0)
+
+    ends = {}
+
+    def put_padded(i, value):
+        put(i, value)
+        first = ends.setdefault("first", value)
+        if i < LOW_PAD:
+            padded_ref[pl.ds(SUB * i, SUB), :] = first
+        if i == count - 1:
+            for k in range(HIGH_PAD):
+                padded_ref[pl.ds(SUB * (LOW_PAD + count + k), SUB), :] = value
+
+    sweep(count, get, put_padded)
 
     for fetch in fetches:
         fetch.wait()
@@ -88,25 +95,35 @@
         width = jnp.where(sublane == r, width_ref[base + r], width)
     level = level_ref[...].astype(jnp.float32)
     gain = LEVEL_SCALE / (width.astype(jnp.float32) * level)
-    rows = [sublane == r for r in range(SUB)]
     less = width - 1
     bits = [(less & 1) != 0, (less & 2) != 0, (less & 4) != 0]
 
+    def shift_block(block):
+        at = SUB * SUB * block
+        for r in range(SUB):
+            shifted_ref[pl.ds(at + r, SUB, stride=SUB), :] = (
+                padded_ref[pl.ds(SUB * starts[r] + r + at, SUB, stride=SUB), :]
+            )
+
     def shifted(i):
-        value = padded_ref[starts[0] + i]
-        for r in range(1, SUB):
-            value = jnp.where(rows[r], padded_ref[starts[r] + i], value)
-        return value
-
-    window = [shifted(i) for i in range(BAND + 1)]
-    ones = [jnp.where(bits[0], window[i + 2], window[i + 1]) for i in range(BAND - 1)]
-    twos = [jnp.where(bits[1], ones[i + 2], ones[i]) for i in range(BAND - 3)]
-    for d in range(count):
-        if d:
+        if i % SUB == 0:
+            shift_block(i // SUB)
+        return shifted_ref[pl.ds(SUB * i, SUB), :]
+
+    held = {}
+
+    def profile(d):
+        if d == 0:
+            window = [shifted(i) for i in range(BAND + 1)]
+            ones = [jnp.where(bits[0], window[i + 2], window[i + 1]) for i in range(BAND - 1)]
+            twos = [jnp.where(bits[1], ones[i + 2], ones[i]) for i in range(BAND - 3)]
+        else:
+            window, ones, twos = held["window"], held["ones"], held["twos"]
             window = window[1:] + [shifted(d + BAND)]
             ones = ones[1:] + [jnp.where(bits[0], window[BAND], window[BAND - 1])]
             twos = twos[1:] + [jnp.where(bits[1], ones[BAND - 2], ones[BAND - 4])]
-        out_ref[d] = (window[0] - jnp.where(bits[2], twos[4], twos[0])) * gain
+        held.update(window=window, ones=ones, twos=twos)
+        return (window[0] - jnp.where(bits[2], twos[4], twos[0])) * gain
 
     def out_put(i, value):
         out_ref[i] = value
@@ -115,7 +132,8 @@
         sweep(count, lambda i: out_ref[i], out_put)
         return carry
 
-    lax.fori_loop(0, DIFFUSE - 1, out_again, 0)
+    sweep(count, profile, out_put)
+    lax.fori_loop(0, DIFFUSE - 2, out_again, 0)
     scale_out = level * (ROOT_STEP / LEVEL_SCALE)
 
     def out_final(i, value):
@@ -134,13 +152,14 @@
         in_specs=[hbm, hbm, hbm, vmem],
         out_specs=vmem,
         scratch_shapes=[
-            pltpu.VMEM((LOW_PAD + count + HIGH_PAD, SUB, LANES), jnp.float32),
+            pltpu.VMEM(((LOW_PAD + count + HIGH_PAD) * SUB, LANES), jnp.float32),
+            pltpu.VMEM(((count + BAND) * SUB, LANES), jnp.float32),
             pltpu.SMEM(depth_offset.shape, jnp.int32),
             pltpu.SMEM(band_width.shape, jnp.int32),
             pltpu.VMEM((SUB, LANES), jnp.int32),
             pltpu.SemaphoreType.DMA((3,)),
         ],
-        compiler_params=pltpu.CompilerParams(vmem_limit_bytes=12 << 20),
+        compiler_params=pltpu.CompilerParams(vmem_limit_bytes=14 << 20),
         name="lines",
     )(depth_offset, band_width, edge_level, lines)
 

time: 72.2 us -> 71.5 us (level)
  Pallas kernels: 7.7 us -> 6.8 us
    pallas_call x1, Pallas kernels: 7.7 us -> 6.8 us  [process_lines(): pl.pallas_call(functools.partial(lines_kernel, count), out_shape=jax.Shap...]
where the time goes in v3:
time: 71.5 us; the launch traced here: 71.3 us
  blocking collectives  51.9 us (73%)
  Pallas kernels  6.8 us (10%)
  starting transfers between devices  3.83 us (5%)
  waiting for transfers between devices  3.38 us (5%)
  local copies, waits for them, and re-layouts  3.05 us (4%)
  other arithmetic  1.74 us (2%)
    all_to_all x1, blocking collectives, exchange(): lax.all_to_all(tiles, 'scan', split_axis=0, concat_axis=0, tiled=True)  28.4 us
    all_to_all x1, blocking collectives, body(): lax.all_to_all(done.reshape(scan_count * held, 1, SUB, LANES), 'scan', sp...  23.5 us
    pallas_call x1, Pallas kernels, process_lines(): pl.pallas_call(functools.partial(lines_kernel, count), out_shape=jax.Shap...  6.8 us
    ppermute x2, starting transfers between devices, after_token(): token = lax.ppermute(token, 'scan', pairs)  3.83 us
    ppermute x2, waiting for transfers between devices, after_token(): token = lax.ppermute(token, 'scan', pairs)  3.38 us
    add x1, other arithmetic, after_token(): return exchange(tiled(frames) + 0.0 * token[0, 0])  1.74 us
    reshape x1, local copies, waits for them, and re-layouts, body(): back.reshape(held, groups, halves, SUB, LANES).transpose(0, 1, 3, 2, 4)  1.53 us
  transfers between devices with their start and end apart: 2, of which 2 were waited for; matrix products, arithmetic and copies ran while one was open for 0% of the time, Pallas kernels for 0%

profile of v3, /device:TPU:64, one launch (start us, length us, event | category | flops | bytes accessed | tf_op | source)
XLA Modules:
  0.0 71.3 jit_solution(1560230771019919807)
XLA Ops:
  0.0 0.0 copy-start
  0.0 0.0 copy-start.1
  0.0 0.0 copy-start.2
  0.0 39.4 %conditional.1 = (f32[512,8,128]{2,1,0:T(8,128)S(1)}) conditional(s32[]{:T(128)} %convert_element_type.3, f32[16,128,256]{2,1,0:T(8,128)} %param.6, f32[16,128,256]{2,1,0:T(8,128)} %param.6), branch_computations={%region_0.1_spmd, %region_1.2_spmd} | conditional | flops 524289 | bytes 12623984 | solution.py:190
  0.0 0.8 %slice_bitcast_fusion = f32[8,128]{1,0:T(8,128)S(1)} fusion(f32[16,128,256]{2,1,0:T(8,128)} %param.1), kind=kLoop, calls=%fused_computation.1 | loop fusion | bytes 8192 | tf_op jit(solution)/shard_map/cond/branch_1_fun/squeeze | solution.py:182
  0.8 1.9 %collective-permute-start = (f32[8,128]{1,0:T(8,128)S(1)}, f32[8,128]{1,0:T(8,128)S(1)}, u32[]{:S(2)}, u32[]{:S(2)}) collective-permute-start(f32[8,128]{1,0:T(8,128)S(1)} %slice_bitcast_fusion), channel_id=1, source_target_pairs={{0,8},{8,0},{16,24},{24,16},{32,40},{40,32},{48,56},{56,48},{64,72... | collective-permute-start | bytes 12296 | tf_op jit(solution)/shard_map/cond/branch_1_fun/ppermute | solution.py:184
  2.7 1.7 %collective-permute-done = f32[8,128]{1,0:T(8,128)S(1)} collective-permute-done((f32[8,128]{1,0:T(8,128)S(1)}, f32[8,128]{1,0:T(8,128)S(1)}, u32[]{:S(2)}, u32[]{:S(2)}) %collective-permute-start) | collective-permute-done | bytes 4128 | tf_op jit(solution)/shard_map/cond/branch_1_fun/ppermute | solution.py:184
  4.4 1.9 %collective-permute-start.1 = (f32[8,128]{1,0:T(8,128)S(1)}, f32[8,128]{1,0:T(8,128)S(1)}, u32[]{:S(2)}, u32[]{:S(2)}) collective-permute-start(f32[8,128]{1,0:T(8,128)S(1)} %collective-permute-done), channel_id=1, source_target_pairs={{0,8},{8,0},{16,24},{24,16},{32,40},{40,32},{48,56},{56,48},{64,72... | collective-permute-start | bytes 12296 | tf_op jit(solution)/shard_map/cond/branch_1_fun/ppermute | solution.py:184
  6.3 1.7 %collective-permute-done.1 = f32[8,128]{1,0:T(8,128)S(1)} collective-permute-done((f32[8,128]{1,0:T(8,128)S(1)}, f32[8,128]{1,0:T(8,128)S(1)}, u32[]{:S(2)}, u32[]{:S(2)}) %collective-permute-start.1) | collective-permute-done | bytes 4128 | tf_op jit(solution)/shard_map/cond/branch_1_fun/ppermute | solution.py:184
  8.0 0.5 slice.5
  9.1 1.7 %add_bitcast_fusion = f32[16,2,16,8,128]{4,3,1,0,2:T(8,128)S(1)} fusion(f32[16,128,256]{2,1,0:T(8,128)} %param.1, f32[]{:T(128)} %bitcast.6), kind=kLoop, calls=%fused_computation | loop fusion | flops 524288 | bytes 4194308 | tf_op jit(solution)/shard_map/cond/branch_1_fun/add | solution.py:185
  10.8 0.2 copy.9
  11.1 28.4 %all_to_all.24 = f32[32,16,8,128]{3,2,1,0:T(8,128)S(1)} all-to-all(f32[32,16,8,128]{3,2,1,0:T(8,128)S(1)} %bitcast.31), channel_id=1, replica_groups=mesh['scan'=32,'col'=8] {'scan'}, dimensions={0} | all-to-all | bytes 4194304 | tf_op jit(solution)/shard_map/cond/branch_1_fun/all_to_all | solution.py:178
  39.4 0.0 copy-done
  39.5 0.0 copy-done.1
  39.5 0.0 copy-done.2
  39.5 6.8 %lines.1 = f32[512,8,128]{2,1,0:T(8,128)S(1)} custom-call(s32[128]{0:T(128)S(1)} %copy-done.1, s32[128]{0:T(128)S(1)} %copy-done.2, s32[128,256]{1,0:T(8,128)S(1)} %copy-done, f32[512,8,128]{2,1,0:T(8,128)S(1)} %get-tuple-element.11.lines_ref), custom_call_target="tpu_custom_call" | custom-call | tf_op jit(solution)/shard_map/lines/pallas_call | solution.py:149
  46.3 23.5 %all_to_all.25 = f32[512,1,8,128]{3,2,1,0:T(8,128)S(1)} all-to-all(f32[512,1,8,128]{3,2,1,0:T(8,128)S(1)} %bitcast.27), channel_id=1, replica_groups=mesh['scan'=32,'col'=8] {'scan'}, dimensions={0} | all-to-all | bytes 4194304 | tf_op jit(solution)/shard_map/all_to_all | solution.py:193
  69.8 1.5 %copy.13 = f32[16,16,2,8,128]{4,3,2,1,0:T(8,128)} copy(f32[16,16,2,8,128]{4,3,0,2,1:T(8,128)S(1)} %bitcast.32) | data formatting | bytes 4194304 | tf_op jit(solution)/shard_map/reshape | solution.py:194
Async XLA Ops:
  0.0 39.4 %copy-start = (s32[128,256]{1,0:T(8,128)S(1)}, s32[128,256]{1,0:T(8,128)}, u32[]{:S(2)}) copy-start(s32[128,256]{1,0:T(8,128)} %level_hbm.1) | copy-start | bytes 393220
  0.0 39.4 %copy-start.1 = (s32[128]{0:T(128)S(1)}, s32[128]{0:T(128)}, u32[]{:S(2)}) copy-start(s32[128]{0:T(128)} %offset_hbm.1) | copy-start | bytes 1540
  0.0 39.5 %copy-start.2 = (s32[128]{0:T(128)S(1)}, s32[128]{0:T(128)}, u32[]{:S(2)}) copy-start(s32[128]{0:T(128)} %width_hbm.1) | copy-start | bytes 1540
  0.8 3.6 %collective-permute-start = (f32[8,128]{1,0:T(8,128)S(1)}, f32[8,128]{1,0:T(8,128)S(1)}, u32[]{:S(2)}, u32[]{:S(2)}) collective-permute-start(f32[8,128]{1,0:T(8,128)S(1)} %slice_bitcast_fusion), channel_id=1, source_target_pairs={{0,8},{8,0},{16,24},{24,16},{32,40},{40,32},{48,56},{56,48},{64,72... | collective-permute-start | bytes 12296 | tf_op jit(solution)/shard_map/cond/branch_1_fun/ppermute | solution.py:184
  4.4 3.6 %collective-permute-start.1 = (f32[8,128]{1,0:T(8,128)S(1)}, f32[8,128]{1,0:T(8,128)S(1)}, u32[]{:S(2)}, u32[]{:S(2)}) collective-permute-start(f32[8,128]{1,0:T(8,128)S(1)} %collective-permute-done), channel_id=1, source_target_pairs={{0,8},{8,0},{16,24},{24,16},{32,40},{40,32},{48,56},{56,48},{64,72... | collective-permute-start | bytes 12296 | tf_op jit(solution)/shard_map/cond/branch_1_fun/ppermute | solution.py:184

commit v4 on v3

--- a/solution.py
+++ b/solution.py
@@ -152,8 +152,8 @@
         in_specs=[hbm, hbm, hbm, vmem],
         out_specs=vmem,
         scratch_shapes=[
-            pltpu.VMEM(((LOW_PAD + count + HIGH_PAD) * SUB, LANES), jnp.float32),
-            pltpu.VMEM(((count + BAND) * SUB, LANES), jnp.float32),
+            pltpu.VMEM(((LOW_PAD + count + HIGH_PAD + 1) * SUB, LANES), jnp.float32),
+            pltpu.VMEM(((count + BAND + 1) * SUB, LANES), jnp.float32),
             pltpu.SMEM(depth_offset.shape, jnp.int32),
             pltpu.SMEM(band_width.shape, jnp.int32),
             pltpu.VMEM((SUB, LANES), jnp.int32),
@@ -179,10 +179,10 @@
 
     def after_token(frames):
         pairs = [(p, p ^ 1) for p in range(scan_count)]
-        token = frames[0, :SUB, :LANES]
+        token = frames[:4, :SUB, :LANES]
         for _ in range(HANDOVERS):
             token = lax.ppermute(token, "scan", pairs)
-        return exchange(tiled(frames) + 0.0 * token[0, 0])
+        return exchange(tiled(frames) + 0.0 * token[0, 0, 0])
 
     def at_once(frames):
         return exchange(tiled(frames))

time: 71.5 us -> 70.5 us (0.986)
  blocking collectives: 51.9 us -> 50.5 us
    all_to_all x1, blocking collectives: 23.5 us -> 22.5 us  [body(): lax.all_to_all(done.reshape(scan_count * held, 1, SUB, LANES), 'scan', sp...]
    slice x1 -> x2, local copies, waits for them, and re-layouts: 0.5 us -> 1.29 us  [the longest x1 0.79 us: after_token(): token = frames[:4, :SUB, :LANES]]
    squeeze x1 -> x0, local copies, waits for them, and re-layouts: 0.75 us -> none  [after_token(): token = frames[0, :SUB, :LANES]]
where the time goes in v4:
time: 70.5 us; the launch traced here: 70.3 us
  blocking collectives  50.5 us (72%)
  Pallas kernels  6.8 us (10%)
  starting transfers between devices  3.83 us (5%)
  waiting for transfers between devices  3.64 us (5%)
  local copies, waits for them, and re-layouts  3.08 us (4%)
  other arithmetic  1.74 us (2%)
    all_to_all x1, blocking collectives, exchange(): lax.all_to_all(tiles, 'scan', split_axis=0, concat_axis=0, tiled=True)  28.1 us
    all_to_all x1, blocking collectives, body(): lax.all_to_all(done.reshape(scan_count * held, 1, SUB, LANES), 'scan', sp...  22.5 us
    pallas_call x1, Pallas kernels, process_lines(): pl.pallas_call(functools.partial(lines_kernel, count), out_shape=jax.Shap...  6.8 us
    ppermute x2, starting transfers between devices, after_token(): token = lax.ppermute(token, 'scan', pairs)  3.83 us
    ppermute x2, waiting for transfers between devices, after_token(): token = lax.ppermute(token, 'scan', pairs)  3.64 us
    add x1, other arithmetic, after_token(): return exchange(tiled(frames) + 0.0 * token[0, 0, 0])  1.74 us
    reshape x1, local copies, waits for them, and re-layouts, body(): back.reshape(held, groups, halves, SUB, LANES).transpose(0, 1, 3, 2, 4)  1.53 us
  transfers between devices with their start and end apart: 2, of which 2 were waited for; matrix products, arithmetic and copies ran while one was open for 0% of the time, Pallas kernels for 0%

profile of v4, /device:TPU:64, one launch (start us, length us, event | category | flops | bytes accessed | tf_op | source)
XLA Modules:
  0.0 70.3 jit_solution(1576123846678259564)
XLA Ops:
  0.0 0.0 copy-start
  0.0 0.0 copy-start.1
  0.0 0.0 copy-start.2
  0.0 39.4 %conditional.1 = (f32[512,8,128]{2,1,0:T(8,128)S(1)}) conditional(s32[]{:T(128)} %convert_element_type.3, f32[16,128,256]{2,1,0:T(8,128)} %param.6, f32[16,128,256]{2,1,0:T(8,128)} %param.6), branch_computations={%region_0.1_spmd, %region_1.2_spmd} | conditional | flops 524289 | bytes 12746864 | solution.py:190
  0.0 0.8 %slice.4 = f32[4,8,128]{2,1,0:T(8,128)S(1)} slice(f32[16,128,256]{2,1,0:T(8,128)} %param.1), slice={[0:4], [0:8], [0:128]} | slice | bytes 32768 | tf_op jit(solution)/shard_map/cond/branch_1_fun/slice | solution.py:182
  0.8 1.9 %collective-permute-start = (f32[4,8,128]{2,1,0:T(8,128)S(1)}, f32[4,8,128]{2,1,0:T(8,128)S(1)}, u32[]{:S(2)}, u32[]{:S(2)}) collective-permute-start(f32[4,8,128]{2,1,0:T(8,128)S(1)} %slice.4), channel_id=1, source_target_pairs={{0,8},{8,0},{16,24},{24,16},{32,40},{40,32},{48,56},{56,48},{64,72... | collective-permute-start | bytes 49160 | tf_op jit(solution)/shard_map/cond/branch_1_fun/ppermute | solution.py:184
  2.7 1.8 %collective-permute-done = f32[4,8,128]{2,1,0:T(8,128)S(1)} collective-permute-done((f32[4,8,128]{2,1,0:T(8,128)S(1)}, f32[4,8,128]{2,1,0:T(8,128)S(1)}, u32[]{:S(2)}, u32[]{:S(2)}) %collective-permute-start) | collective-permute-done | bytes 16416 | tf_op jit(solution)/shard_map/cond/branch_1_fun/ppermute | solution.py:184
  4.6 1.9 %collective-permute-start.1 = (f32[4,8,128]{2,1,0:T(8,128)S(1)}, f32[4,8,128]{2,1,0:T(8,128)S(1)}, u32[]{:S(2)}, u32[]{:S(2)}) collective-permute-start(f32[4,8,128]{2,1,0:T(8,128)S(1)} %collective-permute-done), channel_id=1, source_target_pairs={{0,8},{8,0},{16,24},{24,16},{32,40},{40,32},{48,56},{56,48},{64,72... | collective-permute-start | bytes 49160 | tf_op jit(solution)/shard_map/cond/branch_1_fun/ppermute | solution.py:184
  6.5 1.8 %collective-permute-done.1 = f32[4,8,128]{2,1,0:T(8,128)S(1)} collective-permute-done((f32[4,8,128]{2,1,0:T(8,128)S(1)}, f32[4,8,128]{2,1,0:T(8,128)S(1)}, u32[]{:S(2)}, u32[]{:S(2)}) %collective-permute-start.1) | collective-permute-done | bytes 16416 | tf_op jit(solution)/shard_map/cond/branch_1_fun/ppermute | solution.py:184
  8.3 0.5 slice.6
  9.4 1.7 %add_bitcast_fusion = f32[16,2,16,8,128]{4,3,1,0,2:T(8,128)S(1)} fusion(f32[16,128,256]{2,1,0:T(8,128)} %param.1, f32[]{:T(128)} %bitcast.5), kind=kLoop, calls=%fused_computation | loop fusion | flops 524288 | bytes 4194308 | tf_op jit(solution)/shard_map/cond/branch_1_fun/add | solution.py:185
  11.1 0.2 copy.9
  11.4 28.1 %all_to_all.24 = f32[32,16,8,128]{3,2,1,0:T(8,128)S(1)} all-to-all(f32[32,16,8,128]{3,2,1,0:T(8,128)S(1)} %bitcast.29), channel_id=1, replica_groups=mesh['scan'=32,'col'=8] {'scan'}, dimensions={0} | all-to-all | bytes 4194304 | tf_op jit(solution)/shard_map/cond/branch_1_fun/all_to_all | solution.py:178
  39.4 0.0 copy-done
  39.5 0.0 copy-done.1
  39.5 0.0 copy-done.2
  39.5 6.8 %lines.1 = f32[512,8,128]{2,1,0:T(8,128)S(1)} custom-call(s32[128]{0:T(128)S(1)} %copy-done.1, s32[128]{0:T(128)S(1)} %copy-done.2, s32[128,256]{1,0:T(8,128)S(1)} %copy-done, f32[512,8,128]{2,1,0:T(8,128)S(1)} %get-tuple-element.11.lines_ref), custom_call_target="tpu_custom_call" | custom-call | tf_op jit(solution)/shard_map/lines/pallas_call | solution.py:149
  46.3 22.5 %all_to_all.25 = f32[512,1,8,128]{3,2,1,0:T(8,128)S(1)} all-to-all(f32[512,1,8,128]{3,2,1,0:T(8,128)S(1)} %bitcast.25), channel_id=1, replica_groups=mesh['scan'=32,'col'=8] {'scan'}, dimensions={0} | all-to-all | bytes 4194304 | tf_op jit(solution)/shard_map/all_to_all | solution.py:193
  68.7 1.5 %copy.13 = f32[16,16,2,8,128]{4,3,2,1,0:T(8,128)} copy(f32[16,16,2,8,128]{4,3,0,2,1:T(8,128)S(1)} %bitcast.30) | data formatting | bytes 4194304 | tf_op jit(solution)/shard_map/reshape | solution.py:194
Async XLA Ops:
  0.0 39.4 %copy-start = (s32[128,256]{1,0:T(8,128)S(1)}, s32[128,256]{1,0:T(8,128)}, u32[]{:S(2)}) copy-start(s32[128,256]{1,0:T(8,128)} %level_hbm.1) | copy-start | bytes 393220
  0.0 39.4 %copy-start.1 = (s32[128]{0:T(128)S(1)}, s32[128]{0:T(128)}, u32[]{:S(2)}) copy-start(s32[128]{0:T(128)} %offset_hbm.1) | copy-start | bytes 1540
  0.0 39.5 %copy-start.2 = (s32[128]{0:T(128)S(1)}, s32[128]{0:T(128)}, u32[]{:S(2)}) copy-start(s32[128]{0:T(128)} %width_hbm.1) | copy-start | bytes 1540
  0.8 3.7 %collective-permute-start = (f32[4,8,128]{2,1,0:T(8,128)S(1)}, f32[4,8,128]{2,1,0:T(8,128)S(1)}, u32[]{:S(2)}, u32[]{:S(2)}) collective-permute-start(f32[4,8,128]{2,1,0:T(8,128)S(1)} %slice.4), channel_id=1, source_target_pairs={{0,8},{8,0},{16,24},{24,16},{32,40},{40,32},{48,56},{56,48},{64,72... | collective-permute-start | bytes 49160 | tf_op jit(solution)/shard_map/cond/branch_1_fun/ppermute | solution.py:184
  4.6 3.7 %collective-permute-start.1 = (f32[4,8,128]{2,1,0:T(8,128)S(1)}, f32[4,8,128]{2,1,0:T(8,128)S(1)}, u32[]{:S(2)}, u32[]{:S(2)}) collective-permute-start(f32[4,8,128]{2,1,0:T(8,128)S(1)} %collective-permute-done), channel_id=1, source_target_pairs={{0,8},{8,0},{16,24},{24,16},{32,40},{40,32},{48,56},{56,48},{64,72... | collective-permute-start | bytes 49160 | tf_op jit(solution)/shard_map/cond/branch_1_fun/ppermute | solution.py:184

commit v5 on v4

--- a/solution.py
+++ b/solution.py
@@ -164,6 +164,40 @@
     )(depth_offset, band_width, edge_level, lines)
 
 
+def copy_all(copies):
+    for copy in copies:
+        copy.start()
+    for copy in copies:
+        copy.wait()
+
+
+def to_frames_kernel(tiles_ref, frames_ref, sems):
+    copy_all([
+        pltpu.make_async_copy(tiles_ref.at[:, f], frames_ref.at[f], sems.at[f])
+        for f in range(frames_ref.shape[0])
+    ])
+
+
+def to_tiles_kernel(frames_ref, tiles_ref, sems):
+    copy_all([
+        pltpu.make_async_copy(frames_ref.at[f], tiles_ref.at[:, f], sems.at[f])
+        for f in range(frames_ref.shape[0])
+    ])
+
+
+def relayout(kernel, value, source, target, name):
+    shape = (value.shape[1], value.shape[0]) + value.shape[2:]
+    return pl.pallas_call(
+        kernel,
+        out_shape=jax.ShapeDtypeStruct(shape, value.dtype),
+        in_specs=[pl.BlockSpec(memory_space=source)],
+        out_specs=pl.BlockSpec(memory_space=target),
+        scratch_shapes=[pltpu.SemaphoreType.DMA((min(shape[:2]),))],
+        compiler_params=pltpu.CompilerParams(vmem_limit_bytes=6 << 20),
+        name=name,
+    )(value)
+
+
 def body(frames, depth_offset, band_width, edge_level):
     scan_count = lax.axis_size("scan")
     held, rows, cols = frames.shape
@@ -185,12 +219,16 @@
         return exchange(tiled(frames) + 0.0 * token[0, 0, 0])
 
     def at_once(frames):
-        return exchange(tiled(frames))
+        tiles = frames.reshape(held, groups, SUB, halves, LANES).transpose(0, 1, 3, 2, 4)
+        tiles = tiles.reshape(held, scan_count, SUB, LANES)
+        tiles = pltpu.with_memory_space_constraint(tiles, pltpu.HBM)
+        return exchange(relayout(to_tiles_kernel, tiles, pltpu.HBM, pltpu.VMEM, "to_tiles"))
 
     lines = lax.cond(lax.axis_index("col") % 2 == 0, after_token, at_once, frames)
     lines = lines.reshape(scan_count * held, SUB, LANES)
     done = process_lines(lines, depth_offset, band_width, edge_level)
-    back = lax.all_to_all(done.reshape(scan_count * held, 1, SUB, LANES), "scan", split_axis=0, concat_axis=1, tiled=True)
+    back = exchange(done.reshape(scan_count, held, SUB, LANES))
+    back = relayout(to_frames_kernel, back, pltpu.VMEM, pltpu.HBM, "to_frames")
     back = back.reshape(held, groups, halves, SUB, LANES).transpose(0, 1, 3, 2, 4)
     return back.reshape(held, rows, cols)
 

time: 70.5 us -> 70.3 us (level)
  local copies, waits for them, and re-layouts: 3.08 us -> 1.55 us
  Pallas kernels: 6.8 us -> 8.24 us
    all_to_all x1 -> x0, blocking collectives: 22.5 us -> none  [body(): lax.all_to_all(done.reshape(scan_count * held, 1, SUB, LANES), 'scan', sp...]
    all_to_all x1 -> x2, blocking collectives: 28.1 us -> 50.4 us  [exchange(): lax.all_to_all(tiles, 'scan', split_axis=0, concat_axis=0, tiled=True)]
    reshape x1 -> x0, local copies, waits for them, and re-layouts: 1.53 us -> none  [body(): back.reshape(held, groups, halves, SUB, LANES).transpose(0, 1, 3, 2, 4)]
    pallas_call x0 -> x1, Pallas kernels: none -> 1.44 us  [relayout(): pl.pallas_call(kernel, out_shape=jax.ShapeDtypeStruct(shape, value.dtype)...]
where the time goes in v5:
time: 70.3 us; the launch traced here: 70.1 us
  blocking collectives  50.4 us (72%)
  Pallas kernels  8.24 us (12%)
  starting transfers between devices  3.83 us (5%)
  waiting for transfers between devices  3.64 us (5%)
  other arithmetic  1.74 us (2%)
  local copies, waits for them, and re-layouts  1.55 us (2%)
    all_to_all x2, blocking collectives, exchange(): lax.all_to_all(tiles, 'scan', split_axis=0, concat_axis=0, tiled=True)  50.4 us
    pallas_call x1, Pallas kernels, process_lines(): pl.pallas_call(functools.partial(lines_kernel, count), out_shape=jax.Shap...  6.8 us
    ppermute x2, starting transfers between devices, after_token(): token = lax.ppermute(token, 'scan', pairs)  3.83 us
    ppermute x2, waiting for transfers between devices, after_token(): token = lax.ppermute(token, 'scan', pairs)  3.64 us
    add x1, other arithmetic, after_token(): return exchange(tiled(frames) + 0.0 * token[0, 0, 0])  1.74 us
    pallas_call x1, Pallas kernels, relayout(): pl.pallas_call(kernel, out_shape=jax.ShapeDtypeStruct(shape, value.dtype)...  1.44 us
  transfers between devices with their start and end apart: 2, of which 2 were waited for; matrix products, arithmetic and copies ran while one was open for 0% of the time, Pallas kernels for 0%

profile of v5, /device:TPU:64, one launch (start us, length us, event | category | flops | bytes accessed | tf_op | source)
XLA Modules:
  0.0 70.1 jit_solution(8919095816360184857)
XLA Ops:
  0.0 0.0 copy-start
  0.0 0.0 copy-start.1
  0.0 0.0 copy-start.2
  0.0 39.3 %conditional.1 = (f32[512,8,128]{2,1,0:T(8,128)S(1)}) conditional(s32[]{:T(128)} %convert_element_type.3, f32[16,128,256]{2,1,0:T(8,128)} %param.6, f32[16,128,256]{2,1,0:T(8,128)} %param.6), branch_computations={%region_0.1_spmd, %region_1.2_spmd} | conditional | flops 524289 | bytes 12746864 | solution.py:227
  0.0 0.8 %slice.4 = f32[4,8,128]{2,1,0:T(8,128)S(1)} slice(f32[16,128,256]{2,1,0:T(8,128)} %param.1), slice={[0:4], [0:8], [0:128]} | slice | bytes 32768 | tf_op jit(solution)/shard_map/cond/branch_1_fun/slice | solution.py:216
  0.8 1.9 %collective-permute-start = (f32[4,8,128]{2,1,0:T(8,128)S(1)}, f32[4,8,128]{2,1,0:T(8,128)S(1)}, u32[]{:S(2)}, u32[]{:S(2)}) collective-permute-start(f32[4,8,128]{2,1,0:T(8,128)S(1)} %slice.4), channel_id=1, source_target_pairs={{0,8},{8,0},{16,24},{24,16},{32,40},{40,32},{48,56},{56,48},{64,72... | collective-permute-start | bytes 49160 | tf_op jit(solution)/shard_map/cond/branch_1_fun/ppermute | solution.py:218
  2.7 1.8 %collective-permute-done = f32[4,8,128]{2,1,0:T(8,128)S(1)} collective-permute-done((f32[4,8,128]{2,1,0:T(8,128)S(1)}, f32[4,8,128]{2,1,0:T(8,128)S(1)}, u32[]{:S(2)}, u32[]{:S(2)}) %collective-permute-start) | collective-permute-done | bytes 16416 | tf_op jit(solution)/shard_map/cond/branch_1_fun/ppermute | solution.py:218
  4.6 1.9 %collective-permute-start.1 = (f32[4,8,128]{2,1,0:T(8,128)S(1)}, f32[4,8,128]{2,1,0:T(8,128)S(1)}, u32[]{:S(2)}, u32[]{:S(2)}) collective-permute-start(f32[4,8,128]{2,1,0:T(8,128)S(1)} %collective-permute-done), channel_id=1, source_target_pairs={{0,8},{8,0},{16,24},{24,16},{32,40},{40,32},{48,56},{56,48},{64,72... | collective-permute-start | bytes 49160 | tf_op jit(solution)/shard_map/cond/branch_1_fun/ppermute | solution.py:218
  6.5 1.8 %collective-permute-done.1 = f32[4,8,128]{2,1,0:T(8,128)S(1)} collective-permute-done((f32[4,8,128]{2,1,0:T(8,128)S(1)}, f32[4,8,128]{2,1,0:T(8,128)S(1)}, u32[]{:S(2)}, u32[]{:S(2)}) %collective-permute-start.1) | collective-permute-done | bytes 16416 | tf_op jit(solution)/shard_map/cond/branch_1_fun/ppermute | solution.py:218
  8.3 0.5 slice.6
  9.4 1.7 %add_bitcast_fusion = f32[16,2,16,8,128]{4,3,1,0,2:T(8,128)S(1)} fusion(f32[16,128,256]{2,1,0:T(8,128)} %param.1, f32[]{:T(128)} %bitcast.6), kind=kLoop, calls=%fused_computation | loop fusion | flops 524288 | bytes 4194308 | tf_op jit(solution)/shard_map/cond/branch_1_fun/add | solution.py:219
  11.1 0.2 copy.5
  11.4 28.0 %all_to_all.14 = f32[32,16,8,128]{3,2,1,0:T(8,128)S(1)} all-to-all(f32[32,16,8,128]{3,2,1,0:T(8,128)S(1)} %bitcast.23), channel_id=1, replica_groups=mesh['scan'=32,'col'=8] {'scan'}, dimensions={0} | all-to-all | bytes 4194304 | tf_op jit(solution)/shard_map/cond/branch_1_fun/all_to_all | solution.py:212
  39.3 0.0 copy-done
  39.3 0.0 copy-done.1
  39.3 0.0 copy-done.2
  39.3 6.8 %lines.1 = f32[512,8,128]{2,1,0:T(8,128)S(1)} custom-call(s32[128]{0:T(128)S(1)} %copy-done.1, s32[128]{0:T(128)S(1)} %copy-done.2, s32[128,256]{1,0:T(8,128)S(1)} %copy-done, f32[512,8,128]{2,1,0:T(8,128)S(1)} %get-tuple-element.11.lines_ref), custom_call_target="tpu_custom_call" | custom-call | tf_op jit(solution)/shard_map/lines/pallas_call | solution.py:149
  46.2 22.5 %all_to_all.15.tiles_ref = f32[32,16,8,128]{3,2,1,0:T(8,128)S(1)} all-to-all(f32[32,16,8,128]{3,2,1,0:T(8,128)S(1)} %bitcast.19), channel_id=1, replica_groups=mesh['scan'=32,'col'=8] {'scan'}, dimensions={0} | all-to-all | bytes 4194304 | tf_op jit(solution)/shard_map/all_to_all | solution.py:212
  68.6 1.4 %to_frames.1 = f32[16,32,8,128]{3,2,1,0:T(8,128)} custom-call(f32[32,16,8,128]{3,2,1,0:T(8,128)S(1)} %all_to_all.15.tiles_ref), custom_call_target="tpu_custom_call" | custom-call | tf_op jit(solution)/shard_map/to_frames/pallas_call | solution.py:190
Async XLA Ops:
  0.0 39.3 %copy-start = (s32[128,256]{1,0:T(8,128)S(1)}, s32[128,256]{1,0:T(8,128)}, u32[]{:S(2)}) copy-start(s32[128,256]{1,0:T(8,128)} %level_hbm.1) | copy-start | bytes 393220
  0.0 39.3 %copy-start.1 = (s32[128]{0:T(128)S(1)}, s32[128]{0:T(128)}, u32[]{:S(2)}) copy-start(s32[128]{0:T(128)} %offset_hbm.1) | copy-start | bytes 1540
  0.0 39.3 %copy-start.2 = (s32[128]{0:T(128)S(1)}, s32[128]{0:T(128)}, u32[]{:S(2)}) copy-start(s32[128]{0:T(128)} %width_hbm.1) | copy-start | bytes 1540
  0.8 3.7 %collective-permute-start = (f32[4,8,128]{2,1,0:T(8,128)S(1)}, f32[4,8,128]{2,1,0:T(8,128)S(1)}, u32[]{:S(2)}, u32[]{:S(2)}) collective-permute-start(f32[4,8,128]{2,1,0:T(8,128)S(1)} %slice.4), channel_id=1, source_target_pairs={{0,8},{8,0},{16,24},{24,16},{32,40},{40,32},{48,56},{56,48},{64,72... | collective-permute-start | bytes 49160 | tf_op jit(solution)/shard_map/cond/branch_1_fun/ppermute | solution.py:218
  4.6 3.7 %collective-permute-start.1 = (f32[4,8,128]{2,1,0:T(8,128)S(1)}, f32[4,8,128]{2,1,0:T(8,128)S(1)}, u32[]{:S(2)}, u32[]{:S(2)}) collective-permute-start(f32[4,8,128]{2,1,0:T(8,128)S(1)} %collective-permute-done), channel_id=1, source_target_pairs={{0,8},{8,0},{16,24},{24,16},{32,40},{40,32},{48,56},{56,48},{64,72... | collective-permute-start | bytes 49160 | tf_op jit(solution)/shard_map/cond/branch_1_fun/ppermute | solution.py:218

commit v6 on v5

--- a/solution.py
+++ b/solution.py
@@ -70,7 +70,7 @@
         sweep(count, get, put)
         return carry
 
-    lax.fori_loop(0, SWEEPS - 2, again, 0)
+    lax.fori_loop(0, SWEEPS - 2, again, 0, unroll=2)
 
     ends = {}
 
@@ -133,7 +133,7 @@
         return carry
 
     sweep(count, profile, out_put)
-    lax.fori_loop(0, DIFFUSE - 2, out_again, 0)
+    lax.fori_loop(0, DIFFUSE - 2, out_again, 0, unroll=2)
     scale_out = level * (ROOT_STEP / LEVEL_SCALE)
 
     def out_final(i, value):

time: 70.3 us -> 70.2 us (level)
  no operation moved by 1% of the time
where the time goes in v6:
time: 70.2 us; the launch traced here: 70 us
  blocking collectives  50.4 us (72%)
  Pallas kernels  8.2 us (12%)
  starting transfers between devices  3.83 us (5%)
  waiting for transfers between devices  3.64 us (5%)
  other arithmetic  1.74 us (2%)
  local copies, waits for them, and re-layouts  1.55 us (2%)
    all_to_all x2, blocking collectives, exchange(): lax.all_to_all(tiles, 'scan', split_axis=0, concat_axis=0, tiled=True)  50.4 us
    pallas_call x1, Pallas kernels, process_lines(): pl.pallas_call(functools.partial(lines_kernel, count), out_shape=jax.Shap...  6.76 us
    ppermute x2, starting transfers between devices, after_token(): token = lax.ppermute(token, 'scan', pairs)  3.83 us
    ppermute x2, waiting for transfers between devices, after_token(): token = lax.ppermute(token, 'scan', pairs)  3.64 us
    add x1, other arithmetic, after_token(): return exchange(tiled(frames) + 0.0 * token[0, 0, 0])  1.74 us
    pallas_call x1, Pallas kernels, relayout(): pl.pallas_call(kernel, out_shape=jax.ShapeDtypeStruct(shape, value.dtype)...  1.44 us
  transfers between devices with their start and end apart: 2, of which 2 were waited for; matrix products, arithmetic and copies ran while one was open for 0% of the time, Pallas kernels for 0%

profile of v6, /device:TPU:64, one launch (start us, length us, event | category | flops | bytes accessed | tf_op | source)
XLA Modules:
  0.0 70.0 jit_solution(3454329622401428238)
XLA Ops:
  0.0 0.0 copy-start
  0.0 0.0 copy-start.1
  0.0 0.0 copy-start.2
  0.0 39.3 %conditional.1 = (f32[512,8,128]{2,1,0:T(8,128)S(1)}) conditional(s32[]{:T(128)} %convert_element_type.3, f32[16,128,256]{2,1,0:T(8,128)} %param.6, f32[16,128,256]{2,1,0:T(8,128)} %param.6), branch_computations={%region_0.1_spmd, %region_1.2_spmd} | conditional | flops 524289 | bytes 12746864 | solution.py:227
  0.0 0.8 %slice.4 = f32[4,8,128]{2,1,0:T(8,128)S(1)} slice(f32[16,128,256]{2,1,0:T(8,128)} %param.1), slice={[0:4], [0:8], [0:128]} | slice | bytes 32768 | tf_op jit(solution)/shard_map/cond/branch_1_fun/slice | solution.py:216
  0.8 1.9 %collective-permute-start = (f32[4,8,128]{2,1,0:T(8,128)S(1)}, f32[4,8,128]{2,1,0:T(8,128)S(1)}, u32[]{:S(2)}, u32[]{:S(2)}) collective-permute-start(f32[4,8,128]{2,1,0:T(8,128)S(1)} %slice.4), channel_id=1, source_target_pairs={{0,8},{8,0},{16,24},{24,16},{32,40},{40,32},{48,56},{56,48},{64,72... | collective-permute-start | bytes 49160 | tf_op jit(solution)/shard_map/cond/branch_1_fun/ppermute | solution.py:218
  2.7 1.8 %collective-permute-done = f32[4,8,128]{2,1,0:T(8,128)S(1)} collective-permute-done((f32[4,8,128]{2,1,0:T(8,128)S(1)}, f32[4,8,128]{2,1,0:T(8,128)S(1)}, u32[]{:S(2)}, u32[]{:S(2)}) %collective-permute-start) | collective-permute-done | bytes 16416 | tf_op jit(solution)/shard_map/cond/branch_1_fun/ppermute | solution.py:218
  4.6 1.9 %collective-permute-start.1 = (f32[4,8,128]{2,1,0:T(8,128)S(1)}, f32[4,8,128]{2,1,0:T(8,128)S(1)}, u32[]{:S(2)}, u32[]{:S(2)}) collective-permute-start(f32[4,8,128]{2,1,0:T(8,128)S(1)} %collective-permute-done), channel_id=1, source_target_pairs={{0,8},{8,0},{16,24},{24,16},{32,40},{40,32},{48,56},{56,48},{64,72... | collective-permute-start | bytes 49160 | tf_op jit(solution)/shard_map/cond/branch_1_fun/ppermute | solution.py:218
  6.5 1.8 %collective-permute-done.1 = f32[4,8,128]{2,1,0:T(8,128)S(1)} collective-permute-done((f32[4,8,128]{2,1,0:T(8,128)S(1)}, f32[4,8,128]{2,1,0:T(8,128)S(1)}, u32[]{:S(2)}, u32[]{:S(2)}) %collective-permute-start.1) | collective-permute-done | bytes 16416 | tf_op jit(solution)/shard_map/cond/branch_1_fun/ppermute | solution.py:218
  8.3 0.5 slice.6
  9.4 1.7 %add_bitcast_fusion = f32[16,2,16,8,128]{4,3,1,0,2:T(8,128)S(1)} fusion(f32[16,128,256]{2,1,0:T(8,128)} %param.1, f32[]{:T(128)} %bitcast.6), kind=kLoop, calls=%fused_computation | loop fusion | flops 524288 | bytes 4194308 | tf_op jit(solution)/shard_map/cond/branch_1_fun/add | solution.py:219
  11.1 0.2 copy.5
  11.4 28.0 %all_to_all.14 = f32[32,16,8,128]{3,2,1,0:T(8,128)S(1)} all-to-all(f32[32,16,8,128]{3,2,1,0:T(8,128)S(1)} %bitcast.23), channel_id=1, replica_groups=mesh['scan'=32,'col'=8] {'scan'}, dimensions={0} | all-to-all | bytes 4194304 | tf_op jit(solution)/shard_map/cond/branch_1_fun/all_to_all | solution.py:212
  39.3 0.0 copy-done
  39.3 0.0 copy-done.1
  39.3 0.0 copy-done.2
  39.3 6.8 %lines.1 = f32[512,8,128]{2,1,0:T(8,128)S(1)} custom-call(s32[128]{0:T(128)S(1)} %copy-done.1, s32[128]{0:T(128)S(1)} %copy-done.2, s32[128,256]{1,0:T(8,128)S(1)} %copy-done, f32[512,8,128]{2,1,0:T(8,128)S(1)} %get-tuple-element.11.lines_ref), custom_call_target="tpu_custom_call" | custom-call | tf_op jit(solution)/shard_map/lines/pallas_call | solution.py:149
  46.1 22.5 %all_to_all.15.tiles_ref = f32[32,16,8,128]{3,2,1,0:T(8,128)S(1)} all-to-all(f32[32,16,8,128]{3,2,1,0:T(8,128)S(1)} %bitcast.19), channel_id=1, replica_groups=mesh['scan'=32,'col'=8] {'scan'}, dimensions={0} | all-to-all | bytes 4194304 | tf_op jit(solution)/shard_map/all_to_all | solution.py:212
  68.6 1.4 %to_frames.1 = f32[16,32,8,128]{3,2,1,0:T(8,128)} custom-call(f32[32,16,8,128]{3,2,1,0:T(8,128)S(1)} %all_to_all.15.tiles_ref), custom_call_target="tpu_custom_call" | custom-call | tf_op jit(solution)/shard_map/to_frames/pallas_call | solution.py:190
Async XLA Ops:
  0.0 39.3 %copy-start = (s32[128,256]{1,0:T(8,128)S(1)}, s32[128,256]{1,0:T(8,128)}, u32[]{:S(2)}) copy-start(s32[128,256]{1,0:T(8,128)} %level_hbm.1) | copy-start | bytes 393220
  0.0 39.3 %copy-start.1 = (s32[128]{0:T(128)S(1)}, s32[128]{0:T(128)}, u32[]{:S(2)}) copy-start(s32[128]{0:T(128)} %offset_hbm.1) | copy-start | bytes 1540
  0.0 39.3 %copy-start.2 = (s32[128]{0:T(128)S(1)}, s32[128]{0:T(128)}, u32[]{:S(2)}) copy-start(s32[128]{0:T(128)} %width_hbm.1) | copy-start | bytes 1540
  0.8 3.7 %collective-permute-start = (f32[4,8,128]{2,1,0:T(8,128)S(1)}, f32[4,8,128]{2,1,0:T(8,128)S(1)}, u32[]{:S(2)}, u32[]{:S(2)}) collective-permute-start(f32[4,8,128]{2,1,0:T(8,128)S(1)} %slice.4), channel_id=1, source_target_pairs={{0,8},{8,0},{16,24},{24,16},{32,40},{40,32},{48,56},{56,48},{64,72... | collective-permute-start | bytes 49160 | tf_op jit(solution)/shard_map/cond/branch_1_fun/ppermute | solution.py:218
  4.6 3.7 %collective-permute-start.1 = (f32[4,8,128]{2,1,0:T(8,128)S(1)}, f32[4,8,128]{2,1,0:T(8,128)S(1)}, u32[]{:S(2)}, u32[]{:S(2)}) collective-permute-start(f32[4,8,128]{2,1,0:T(8,128)S(1)} %collective-permute-done), channel_id=1, source_target_pairs={{0,8},{8,0},{16,24},{24,16},{32,40},{40,32},{48,56},{56,48},{64,72... | collective-permute-start | bytes 49160 | tf_op jit(solution)/shard_map/cond/branch_1_fun/ppermute | solution.py:218
